TPU v7x, 32 devices: a whole 2x2x4 slice. The times are simulated.
32 devices in a mesh: fsdp: 8 (over z, y), ctx: 4 (over x, core).
Axes of the slice: x: 2, y: 2, z: 4, core: 2. Of those that a mesh axis runs over, the one named last changes fastest.
Arguments:
- hidden: bfloat16 [8, 1024, 8192], P('fsdp', 'ctx'), may hold values from -400 to 400
- norm_gain: bfloat16 [8192], replicated, may hold values from 0.099609375 to 1.8984375
- w_query: bfloat16 [8192, 1024], P('fsdp'), may hold values from -0.109375 to 0.109375
- w_key: bfloat16 [8192, 128], P('fsdp'), may hold values from -0.109375 to 0.109375
- w_value: bfloat16 [8192, 128], P('fsdp'), may hold values from -0.0625 to 0.0625
- bias_query: bfloat16 [1024], replicated, may hold values from -24 to 24
- bias_key: bfloat16 [128], replicated, may hold values from -9 to 9
- bias_value: bfloat16 [128], replicated, may hold values from -3 to 3
Outputs:
- attended: bfloat16 [8, 1024, 1024], P('fsdp', 'ctx')
All inputs are finite; a program needn't handle non-finite values.
Results may differ from a plain program's by a relative error of at most 0.012.
Values may be sent and summed in bfloat16 or wider, within the bound.
No kernel may reach another device: no remote copies, remote signals or barrier semaphores. Data moves between devices by JAX's collectives and lax.ppermute only.
A program may use at most 128 MiB of HBM per device.

v0:
```python
import math
import jax
import jax.numpy as jnp
from jax import lax
from jax.sharding import PartitionSpec as P

epsilon = 1e-06
rotary_base = 1000000.0
masked_score = -1e30


def shifted(value, axis, steps):
    count = lax.axis_size(axis)
    first, last = (max(0, -steps), min(count, count - steps))
    return lax.ppermute(value, axis, [(source, source + steps) for source in range(first, last)])


def rotary_tables(positions, head_width):
    half_width = head_width // 2
    frequency = jnp.exp(
        -(jnp.arange(half_width, dtype=jnp.float32) * (2.0 / head_width)) * math.log(rotary_base)
    )
    angles = positions.astype(jnp.float32)[:, None] * frequency[None, :]
    return (jnp.cos(angles)[:, None, :], jnp.sin(angles)[:, None, :])


def rotate(tensor, cosine, sine_table):
    half_width = tensor.shape[-1] // 2
    lower_half = tensor[..., :half_width]
    upper_half = tensor[..., half_width:]
    return jnp.concatenate(
        [
            lower_half * cosine - upper_half * sine_table,
            upper_half * cosine + lower_half * sine_table,
        ],
        axis=-1,
    )


def normalize(inputs, norm_gain):
    floats = inputs.astype(jnp.float32)
    scaled = floats * lax.rsqrt(jnp.mean(floats * floats, axis=-1, keepdims=True) + epsilon)
    return (scaled * norm_gain.astype(jnp.float32)).astype(jnp.bfloat16)


def contract_rows(operand, pieces):
    return tuple((jnp.dot(operand, piece, preferred_element_type=jnp.float32) for piece in pieces))


def attend(work_queries, score_scale, running, key_value, visible):
    row_peak, row_total, weighted = running
    scores = (
        jnp.einsum("qhd,kd->hqk", work_queries, key_value[0], preferred_element_type=jnp.float32)
        * score_scale
    )
    scores = jnp.where(visible, scores, masked_score)
    new_peak = jnp.maximum(row_peak, jnp.max(scores, axis=-1))
    factor = jnp.exp(row_peak - new_peak)
    expsum = jnp.exp(scores - new_peak[..., None])
    row_total = row_total * factor + jnp.sum(expsum, axis=-1)
    weights = expsum.astype(jnp.bfloat16)
    weighted = weighted * factor[..., None] + jnp.einsum(
        "hqk,kd->hqd", weights, key_value[1], preferred_element_type=jnp.float32
    )
    return (new_peak, row_total, weighted)


def shards(hidden, norm_gain, w_query, w_key, w_value, bias_query, bias_key, bias_value):
    local_rows = hidden.shape[1]
    head_width = w_key.shape[1]
    query_width = w_query.shape[1]
    query_heads = query_width // head_width
    normed = normalize(hidden[0], norm_gain)
    sums = contract_rows(
        normed,
        (
            lax.all_gather(w_query, "fsdp", axis=0, tiled=True),
            lax.all_gather(w_key, "fsdp", axis=0, tiled=True),
            lax.all_gather(w_value, "fsdp", axis=0, tiled=True),
        ),
    )
    query_sums, key_sums, value_sums = sums
    slab_index = lax.axis_index("ctx")
    slab_count = lax.axis_size("ctx")
    positions = slab_index * local_rows + jnp.arange(local_rows, dtype=jnp.int32)
    cosine, sine_table = rotary_tables(positions, head_width)
    queries = rotate(
        (query_sums + bias_query.astype(jnp.float32)).reshape(local_rows, query_heads, head_width),
        cosine,
        sine_table,
    ).astype(jnp.bfloat16)
    keys = rotate((key_sums + bias_key.astype(jnp.float32))[:, None, :], cosine, sine_table)[
        :, 0, :
    ].astype(jnp.bfloat16)
    values = (value_sums + bias_value.astype(jnp.float32)).astype(jnp.bfloat16)
    score_scale = head_width ** (-0.5)
    start_state = (
        jnp.full((query_heads, local_rows), masked_score, jnp.float32),
        jnp.zeros((query_heads, local_rows), jnp.float32),
        jnp.zeros((query_heads, local_rows, head_width), jnp.float32),
    )
    key_value = jnp.stack([keys, values])
    column_ids = jnp.arange(local_rows, dtype=jnp.int32)
    causal = column_ids[None, :] <= column_ids[:, None]
    running = attend(queries, score_scale, start_state, key_value, causal[None])

    def forward_step(step_number, state):
        held_running, blocks = state
        blocks = shifted(blocks, "ctx", 1)
        visible = step_number <= slab_index
        held_running = attend(queries, score_scale, held_running, blocks, visible)
        return (held_running, blocks)

    running, key_value = lax.fori_loop(1, slab_count, forward_step, (running, key_value))
    row_peak, row_total, weighted = running
    attended = (
        (weighted / row_total[..., None])
        .transpose(1, 0, 2)
        .reshape(local_rows, query_width)
        .astype(jnp.bfloat16)
    )
    return attended[None]


def solution(mesh):
    in_specs = (
        P("fsdp", "ctx", None),
        P(),
        P("fsdp", None),
        P("fsdp", None),
        P("fsdp", None),
        P(),
        P(),
        P(),
    )
    out_specs = P("fsdp", "ctx", None)
    return jax.shard_map(shards, mesh=mesh, in_specs=in_specs, out_specs=out_specs, check_vma=False)
```

profile of v0, /device:TPU:1, one launch (start us, length us, event | category | flops | bytes accessed | tf_op | source)
XLA Modules:
  0.0 384.0 jit_solution(6353027936937991859)
XLA Ops:
  6.6 0.7 all-gather.4.cloned.1.call-update
  7.3 0.7 all-gather.8.cloned.1.call-update
  8.1 0.7 all-gather.6.cloned.1.call-update
  8.9 3.1 fusion.11
  12.0 0.5 multiply_cosine_fusion
  12.6 47.2 %all-gather.4.cloned.1.call-done = bf16[8192,128]{1,0:T(8,128)(2,1)} async-done(((bf16[1024,128]{1,0:T(8,128)(2,1)}), bf16[8192,128]{1,0:T(8,128)(2,1)}) %all-gather.4.cloned.1.call-update) | async-done | bytes 2097168 | tf_op jit(solution)/shard_map/all_gather | solution.py:78
  59.8 4.6 %fusion.17 = f32[256,1,128]{0,2,1:T(8,128)S(1)} fusion(bf16[8192,128]{1,0:T(8,128)(2,1)} %all-gather.4.cloned.1.call-done, f32[128]{0:T(128)S(1)} %convert_element_type.78, bf16[1,256,8192]{2,1,0:T(8,128)(2,1)} %param.10, f32[8192]{0:T(1024)S(1)} %convert_element_type.76, f32[256]{0:T(256)S(1)} %add_rsqrt_fusion), kind=kOutput, calls=%fused_computation.32 | convolution fusion | flops 545292288 | bytes 6456832 | tf_op jit(solution)/shard_map/dot_general | solution.py:47
  64.8 45.0 %all-gather.8.cloned.1.call-done = bf16[8192,128]{1,0:T(8,128)(2,1)} async-done(((bf16[1024,128]{1,0:T(8,128)(2,1)}), bf16[8192,128]{1,0:T(8,128)(2,1)}) %all-gather.8.cloned.1.call-update) | async-done | bytes 2097168 | tf_op jit(solution)/shard_map/all_gather | solution.py:79
  109.7 4.6 %fusion.18 = bf16[256,128]{0,1:T(8,128)(2,1)S(1)} fusion(bf16[8192,128]{1,0:T(8,128)(2,1)} %all-gather.8.cloned.1.call-done, f32[128]{0:T(128)S(1)} %convert_element_type.84, bf16[1,256,8192]{2,1,0:T(8,128)(2,1)} %param.10, f32[8192]{0:T(1024)S(1)} %convert_element_type.76, f32[256]{0:T(256)S(1)} %add_rsqrt_fusion), kind=kOutput, calls=%fused_computation.33 | convolution fusion | flops 545325056 | bytes 6391296 | tf_op jit(solution)/shard_map/dot_general | solution.py:47
  114.5 224.2 %all-gather.6.cloned.1.call-done = bf16[8192,1024]{1,0:T(8,128)(2,1)} async-done(((bf16[1024,1024]{1,0:T(8,128)(2,1)}), bf16[8192,1024]{1,0:T(8,128)(2,1)}) %all-gather.6.cloned.1.call-update) | async-done | bytes 16777232 | tf_op jit(solution)/shard_map/all_gather | solution.py:77
  338.7 9.6 %fusion.16 = f32[32,8,8,128]{3,1,2,0:T(8,128)S(1)} fusion(bf16[8192,1024]{1,0:T(8,128)(2,1)} %all-gather.6.cloned.1.call-done, f32[1024]{0:T(1024)S(1)} %convert_element_type.82, bf16[1,256,8192]{2,1,0:T(8,128)(2,1)} %param.10, f32[8192]{0:T(1024)S(1)} %convert_element_type.76, f32[256]{0:T(256)S(1)} %add_rsqrt_fusion), kind=kOutput, calls=%fused_computation.28 | convolution fusion | flops 4303618048 | bytes 22057984 | tf_op jit(solution)/shard_map/dot_general | solution.py:47
  349.5 0.5 fusion.37
  350.4 0.8 convolution_add_fusion.2
  351.2 24.6 %while.19 = (s32[]{:T(128)}, f32[8,256]{1,0:T(8,128)S(1)}, f32[8,256]{1,0:T(8,128)S(1)}, f32[8,256,128]{2,1,0:T(8,128)S(1)}, bf16[2,256,128]{2,1,0:T(8,128)(2,1)...) while((s32[]{:T(128)}, f32[8,256]{1,0:T(8,128)S(1)}, f32[8,256]{1,0:T(8,128)S(1)}, ...), condition=%wide.region_6.7_spmd, body=%wide.region_3.6_spmd.sunk | while | flops 274731008 | bytes 9961609 | solution.py:114
  351.2 4.0 %collective-permute-start = (bf16[2,256,128]{2,1,0:T(8,128)(2,1)S(1)}, bf16[2,256,128]{2,1,0:T(8,128)(2,1)S(1)}, u32[]{:S(2)}, u32[]{:S(2)}) collective-permute-start(bf16[2,256,128]{2,1,0:T(8,128)(2,1)S(1)} %get-tuple-element.232), channel_id=1, source_target_pairs={{0,1},{1,2},{2,3},{4,5},{5,6},{6,7},{8,9},{9,10},{10,11},{12,13},{... | collective-permute-start | bytes 393224 | tf_op jit(solution)/shard_map/while/body/eval_jaxpr/ppermute | solution.py:15
  355.2 1.9 collective-permute-done
  358.1 1.0 convolution_add_fusion.6
  359.1 4.4 %collective-permute-start = (bf16[2,256,128]{2,1,0:T(8,128)(2,1)S(1)}, bf16[2,256,128]{2,1,0:T(8,128)(2,1)S(1)}, u32[]{:S(2)}, u32[]{:S(2)}) collective-permute-start(bf16[2,256,128]{2,1,0:T(8,128)(2,1)S(1)} %get-tuple-element.232), channel_id=1, source_target_pairs={{0,1},{1,2},{2,3},{4,5},{5,6},{6,7},{8,9},{9,10},{10,11},{12,13},{... | collective-permute-start | bytes 393224 | tf_op jit(solution)/shard_map/while/body/eval_jaxpr/ppermute | solution.py:15
  363.5 1.9 collective-permute-done
  366.4 1.0 convolution_add_fusion.6
  367.5 4.4 %collective-permute-start = (bf16[2,256,128]{2,1,0:T(8,128)(2,1)S(1)}, bf16[2,256,128]{2,1,0:T(8,128)(2,1)S(1)}, u32[]{:S(2)}, u32[]{:S(2)}) collective-permute-start(bf16[2,256,128]{2,1,0:T(8,128)(2,1)S(1)} %get-tuple-element.232), channel_id=1, source_target_pairs={{0,1},{1,2},{2,3},{4,5},{5,6},{6,7},{8,9},{9,10},{10,11},{12,13},{... | collective-permute-start | bytes 393224 | tf_op jit(solution)/shard_map/while/body/eval_jaxpr/ppermute | solution.py:15
  371.8 1.9 collective-permute-done
  374.7 1.0 convolution_add_fusion.6
  376.5 1.0 convert_element_type.89
  (50 shorter events, 5.6 us)
Async XLA Ops:
  6.5 2.2 copy-start
  6.5 2.2 copy-start.1
  6.5 2.3 copy-start.2
  6.5 2.3 copy-start.3
  6.5 53.3 %all-gather.4.cloned.1.call-start = ((), (), s32[]{:S(2)}) async-start(), calls=%async_computation | async-start | bytes 2359296 | tf_op jit(solution)/shard_map/all_gather | solution.py:78
  7.3 102.5 %all-gather.8.cloned.1.call-start = ((), (), s32[]{:S(2)}) async-start(), calls=%async_computation.2 | async-start | bytes 2359296 | tf_op jit(solution)/shard_map/all_gather | solution.py:79
  8.0 330.7 %all-gather.6.cloned.1.call-start = ((), (), s32[]{:S(2)}) async-start(), calls=%async_computation.1 | async-start | bytes 18874368 | tf_op jit(solution)/shard_map/all_gather | solution.py:77
  351.2 6.0 %collective-permute-start = (bf16[2,256,128]{2,1,0:T(8,128)(2,1)S(1)}, bf16[2,256,128]{2,1,0:T(8,128)(2,1)S(1)}, u32[]{:S(2)}, u32[]{:S(2)}) collective-permute-start(bf16[2,256,128]{2,1,0:T(8,128)(2,1)S(1)} %get-tuple-element.232), channel_id=1, source_target_pairs={{0,1},{1,2},{2,3},{4,5},{5,6},{6,7},{8,9},{9,10},{10,11},{12,13},{... | collective-permute-start | bytes 393224 | tf_op jit(solution)/shard_map/while/body/eval_jaxpr/ppermute | solution.py:15
  359.1 6.3 %collective-permute-start = (bf16[2,256,128]{2,1,0:T(8,128)(2,1)S(1)}, bf16[2,256,128]{2,1,0:T(8,128)(2,1)S(1)}, u32[]{:S(2)}, u32[]{:S(2)}) collective-permute-start(bf16[2,256,128]{2,1,0:T(8,128)(2,1)S(1)} %get-tuple-element.232), channel_id=1, source_target_pairs={{0,1},{1,2},{2,3},{4,5},{5,6},{6,7},{8,9},{9,10},{10,11},{12,13},{... | collective-permute-start | bytes 393224 | tf_op jit(solution)/shard_map/while/body/eval_jaxpr/ppermute | solution.py:15
  367.5 6.3 %collective-permute-start = (bf16[2,256,128]{2,1,0:T(8,128)(2,1)S(1)}, bf16[2,256,128]{2,1,0:T(8,128)(2,1)S(1)}, u32[]{:S(2)}, u32[]{:S(2)}) collective-permute-start(bf16[2,256,128]{2,1,0:T(8,128)(2,1)S(1)} %get-tuple-element.232), channel_id=1, source_target_pairs={{0,1},{1,2},{2,3},{4,5},{5,6},{6,7},{8,9},{9,10},{10,11},{12,13},{... | collective-permute-start | bytes 393224 | tf_op jit(solution)/shard_map/while/body/eval_jaxpr/ppermute | solution.py:15
Sparse Core Ops, SparseCore 0:
  9.5 50.2 all-gather.3
  61.9 47.7 all-gather.7
  111.9 226.7 all-gather.5
where the time goes:
time: 384 us
  waiting for transfers between devices  324 us (84%)
  matrix products  24.5 us (6%)
  between operations  13.3 us (3%)
  starting transfers between devices  12.9 us (3%)
  other arithmetic  6.76 us (2%)
    all_gather x1, waiting for transfers between devices, shards(): lax.all_gather(w_query, 'fsdp', axis=0, tiled=True)  224 us
    all_gather x1, waiting for transfers between devices, shards(): lax.all_gather(w_key, 'fsdp', axis=0, tiled=True)  47.2 us
    all_gather x1, waiting for transfers between devices, shards(): lax.all_gather(w_value, 'fsdp', axis=0, tiled=True)  45 us
    dot_general x3, matrix products, contract_rows(): jnp.dot(operand, piece, preferred_element_type=jnp.float32)  18.8 us
    ppermute x3, starting transfers between devices, shifted(): lax.ppermute(value, axis, [(source, source + steps) for source in range(f...  12.8 us
  transfers between devices with their start and end apart: 6, of which 6 were waited for; matrix products, arithmetic and copies ran while one was open for 3% of the time, Pallas kernels for 0%

commit v1 on v0

--- a/solution.py
+++ b/solution.py
@@ -1,3 +1,4 @@
+import functools
 import math
 import jax
 import jax.numpy as jnp
@@ -7,6 +8,39 @@
 epsilon = 1e-06
 rotary_base = 1000000.0
 masked_score = -1e30
+
+
+def report_the_values(z_in, dim_no):
+    big = list(z_in.shape[1:])
+    big[dim_no] *= z_in.shape[0]
+    return jnp.moveaxis(z_in, 0, dim_no).reshape(big)
+
+
+def row_move(xs, named_axis, at_axis):
+    size_here = lax.axis_size(named_axis)
+    ledger = []
+    for rr in range(size_here):
+        ledger.append((rr, (rr + 1) % size_here))
+    series = []
+    for src_i, i in ledger:
+        series.append((i, src_i))
+    piece_next, view_out = ([], [])
+    for nth in range(size_here - 1):
+        if nth % 2 == 0:
+            local_now = lax.ppermute(piece_next[-1] if piece_next else xs, named_axis, ledger)
+            piece_next.append(local_now)
+        else:
+            row_out = lax.ppermute(view_out[-1] if view_out else xs, named_axis, series)
+            view_out.append(row_out)
+    back = jnp.stack([*piece_next[::-1], xs, *view_out])
+    w1 = lax.axis_index(named_axis)
+    wide_out = len(piece_next)
+    part_next = w1 - wide_out
+    back = back[(jnp.arange(size_here) - part_next) % size_here]
+    return report_the_values(back, at_axis)
+
+
+fix_runs = functools.partial(row_move, named_axis="fsdp", at_axis=0)
 
 
 def shifted(value, axis, steps):
@@ -76,7 +110,7 @@
         (
             lax.all_gather(w_query, "fsdp", axis=0, tiled=True),
             lax.all_gather(w_key, "fsdp", axis=0, tiled=True),
-            lax.all_gather(w_value, "fsdp", axis=0, tiled=True),
+            fix_runs(w_value),
         ),
     )
     query_sums, key_sums, value_sums = sums

time: 384 us -> 355 us (0.924)
  waiting for transfers between devices: 324 us -> 266 us
  starting transfers between devices: 12.9 us -> 36.6 us
  local copies, waits for them, and re-layouts: 2.07 us -> 7.34 us
    all_gather x1, waiting for transfers between devices: 47.2 us -> 0.32 us  [shards(): lax.all_gather(w_key, 'fsdp', axis=0, tiled=True)]
    all_gather x1 -> x0, waiting for transfers between devices: 45 us -> none  [shards(): lax.all_gather(w_value, 'fsdp', axis=0, tiled=True)]
    ppermute x0 -> x7, waiting for transfers between devices: none -> 34.1 us  [the longest x4 33.8 us: row_move(): lax.ppermute(piece_next[-1] if piece_next else xs, named_axis, ledger)]
    ppermute x0 -> x7, starting transfers between devices: none -> 23.8 us  [the longest x3 16.5 us: row_move(): row_out = lax.ppermute(view_out[-1] if view_out else xs, named_axis, series)]
  transfers between devices with their start and end apart: 6 -> 12, of which waited for: 6 -> 10; matrix products, arithmetic and copies ran while one was open for 3% -> 5% of each run, Pallas kernels for 0% -> 0%
where the time goes in v1:
time: 355 us
  waiting for transfers between devices  266 us (75%)
  starting transfers between devices  36.6 us (10%)
  matrix products  24.5 us (7%)
  between operations  13.7 us (4%)
  local copies, waits for them, and re-layouts  7.34 us (2%)
  other arithmetic  6.78 us (2%)
    all_gather x1, waiting for transfers between devices, shards(): lax.all_gather(w_query, 'fsdp', axis=0, tiled=True)  224 us
    ppermute x4, waiting for transfers between devices, row_move(): lax.ppermute(piece_next[-1] if piece_next else xs, named_axis, ledger)  33.8 us
    dot_general x3, matrix products, contract_rows(): jnp.dot(operand, piece, preferred_element_type=jnp.float32)  18.8 us
    ppermute x3, starting transfers between devices, row_move(): row_out = lax.ppermute(view_out[-1] if view_out else xs, named_axis, series)  16.5 us
    ppermute x3, starting transfers between devices, shifted(): lax.ppermute(value, axis, [(source, source + steps) for source in range(f...  12.8 us
    ppermute x4, starting transfers between devices, row_move(): lax.ppermute(piece_next[-1] if piece_next else xs, named_axis, ledger)  7.33 us
  transfers between devices with their start and end apart: 12, of which 10 were waited for; matrix products, arithmetic and copies ran while one was open for 5% of the time, Pallas kernels for 0%

profile of v1, /device:TPU:1, one launch (start us, length us, event | category | flops | bytes accessed | tf_op | source)
XLA Modules:
  0.0 354.9 jit_solution(656343743816649998)
XLA Ops:
  8.0 2.1 collective-permute-start.1
  10.1 3.1 collective-permute-start.5
  13.4 7.6 %collective-permute-done.1 = bf16[1024,128]{1,0:T(8,128)(2,1)S(1)} collective-permute-done((bf16[1024,128]{1,0:T(8,128)(2,1)S(1)}, bf16[1024,128]{1,0:T(8,128)(2,1)S(1)}, u32[]{:S(2)}, u32[]{:S(2)}) %collective-permute-start.1) | collective-permute-done | bytes 262176 | tf_op jit(solution)/shard_map/ppermute | solution.py:30
  21.0 2.3 collective-permute-start.2
  23.3 3.1 fusion.13
  26.4 10.7 %collective-permute-done.2 = bf16[1024,128]{1,0:T(8,128)(2,1)S(1)} collective-permute-done((bf16[1024,128]{1,0:T(8,128)(2,1)S(1)}, bf16[1024,128]{1,0:T(8,128)(2,1)S(1)}, u32[]{:S(2)}, u32[]{:S(2)}) %collective-permute-start.2) | collective-permute-done | bytes 262176 | tf_op jit(solution)/shard_map/ppermute | solution.py:30
  37.1 4.2 %collective-permute-start.6 = (bf16[1024,128]{1,0:T(8,128)(2,1)S(1)}, bf16[1024,128]{1,0:T(8,128)(2,1)}, u32[]{:S(2)}, u32[]{:S(2)}) collective-permute-start(bf16[1024,128]{1,0:T(8,128)(2,1)S(1)} %collective-permute-done.5), channel_id=1, source_target_pairs={{4,0},{8,4},{12,8},{16,12},{20,16},{24,20},{28,24},{0,28},{5,1},{9... | collective-permute-start | bytes 786440 | tf_op jit(solution)/shard_map/ppermute | solution.py:33
  41.3 8.7 %collective-permute-done.3 = bf16[1024,128]{1,0:T(8,128)(2,1)S(1)} collective-permute-done((bf16[1024,128]{1,0:T(8,128)(2,1)S(1)}, bf16[1024,128]{1,0:T(8,128)(2,1)S(1)}, u32[]{:S(2)}, u32[]{:S(2)}) %collective-permute-start.3) | collective-permute-done | bytes 262176 | tf_op jit(solution)/shard_map/ppermute | solution.py:30
  50.0 2.9 collective-permute-start.4
  53.6 9.2 %collective-permute-start.7 = (bf16[1024,128]{1,0:T(8,128)(2,1)}, bf16[1024,128]{1,0:T(8,128)(2,1)S(1)}, u32[]{:S(2)}, u32[]{:S(2)}) collective-permute-start(bf16[1024,128]{1,0:T(8,128)(2,1)} %collective-permute-done.6), channel_id=1, source_target_pairs={{4,0},{8,4},{12,8},{16,12},{20,16},{24,20},{28,24},{0,28},{5,1},{9... | collective-permute-start | bytes 786440 | tf_op jit(solution)/shard_map/ppermute | solution.py:33
  62.8 6.8 %collective-permute-done.4 = bf16[1024,128]{1,0:T(8,128)(2,1)} collective-permute-done((bf16[1024,128]{1,0:T(8,128)(2,1)S(1)}, bf16[1024,128]{1,0:T(8,128)(2,1)}, u32[]{:S(2)}, u32[]{:S(2)}) %collective-permute-start.4) | collective-permute-done | bytes 262176 | tf_op jit(solution)/shard_map/ppermute | solution.py:30
  73.1 2.1 gather_fusion
  75.2 4.6 %fusion.38 = bf16[256,128]{0,1:T(8,128)(2,1)S(1)} fusion(bf16[8192,128]{1,0:T(8,128)(2,1)} %bitcast.104, bf16[1,256,8192]{2,1,0:T(8,128)(2,1)} %param.10, f32[8192]{0:T(1024)S(1)} %convert_element_type.84, f32[256]{0:T(256)S(1)} %add_rsqrt_fusion, f32[128]{0:T(128)S(1)} %convert_element_type.95), kind=kOutput, calls=%fused_computation.43 | convolution fusion | flops 545325056 | bytes 6391296 | tf_op jit(solution)/shard_map/dot_general | solution.py:81
  80.1 4.6 %fusion.32 = f32[256,1,128]{0,2,1:T(8,128)S(1)} fusion(bf16[8192,128]{1,0:T(8,128)(2,1)} %all-gather.3.cloned.1.call-done, bf16[1,256,8192]{2,1,0:T(8,128)(2,1)} %param.10, f32[8192]{0:T(1024)S(1)} %convert_element_type.84, f32[256]{0:T(256)S(1)} %add_rsqrt_fusion, f32[128]{0:T(128)S(1)} %convert_element_type.86), kind=kOutput, calls=%fused_computation.41 | convolution fusion | flops 545292288 | bytes 6456832 | tf_op jit(solution)/shard_map/dot_general | solution.py:81
  85.3 224.1 %all-gather.5.cloned.1.call-done = bf16[8192,1024]{1,0:T(8,128)(2,1)} async-done(((bf16[1024,1024]{1,0:T(8,128)(2,1)}), bf16[8192,1024]{1,0:T(8,128)(2,1)}) %all-gather.5.cloned.1.call-update) | async-done | bytes 16777232 | tf_op jit(solution)/shard_map/all_gather | solution.py:111
  309.3 9.6 %fusion.25 = f32[32,8,8,128]{3,1,2,0:T(8,128)S(1)} fusion(bf16[8192,1024]{1,0:T(8,128)(2,1)} %all-gather.5.cloned.1.call-done, bf16[1,256,8192]{2,1,0:T(8,128)(2,1)} %param.10, f32[8192]{0:T(1024)S(1)} %convert_element_type.84, f32[256]{0:T(256)S(1)} %add_rsqrt_fusion, f32[1024]{0:T(1024)S(1)} %convert_element_type.90), kind=kOutput, calls=%fused_computation.37 | convolution fusion | flops 4303618048 | bytes 22057984 | tf_op jit(solution)/shard_map/dot_general | solution.py:81
  321.8 24.6 %while.19 = (s32[]{:T(128)}, f32[8,256]{1,0:T(8,128)S(1)}, f32[8,256]{1,0:T(8,128)S(1)}, f32[8,256,128]{2,1,0:T(8,128)S(1)}, bf16[2,256,128]{2,1,0:T(8,128)(2,1)...) while((s32[]{:T(128)}, f32[8,256]{1,0:T(8,128)S(1)}, f32[8,256]{1,0:T(8,128)S(1)}, ...), condition=%wide.region_6.7_spmd, body=%wide.region_3.6_spmd.sunk | while | flops 274731008 | bytes 9961609 | solution.py:148
  321.8 4.0 %collective-permute-start = (bf16[2,256,128]{2,1,0:T(8,128)(2,1)S(1)}, bf16[2,256,128]{2,1,0:T(8,128)(2,1)S(1)}, u32[]{:S(2)}, u32[]{:S(2)}) collective-permute-start(bf16[2,256,128]{2,1,0:T(8,128)(2,1)S(1)} %get-tuple-element.232), channel_id=1, source_target_pairs={{0,1},{1,2},{2,3},{4,5},{5,6},{6,7},{8,9},{9,10},{10,11},{12,13},{... | collective-permute-start | bytes 393224 | tf_op jit(solution)/shard_map/while/body/eval_jaxpr/ppermute | solution.py:49
  325.8 1.9 collective-permute-done
  329.8 4.4 %collective-permute-start = (bf16[2,256,128]{2,1,0:T(8,128)(2,1)S(1)}, bf16[2,256,128]{2,1,0:T(8,128)(2,1)S(1)}, u32[]{:S(2)}, u32[]{:S(2)}) collective-permute-start(bf16[2,256,128]{2,1,0:T(8,128)(2,1)S(1)} %get-tuple-element.232), channel_id=1, source_target_pairs={{0,1},{1,2},{2,3},{4,5},{5,6},{6,7},{8,9},{9,10},{10,11},{12,13},{... | collective-permute-start | bytes 393224 | tf_op jit(solution)/shard_map/while/body/eval_jaxpr/ppermute | solution.py:49
  334.1 1.9 collective-permute-done
  338.1 4.4 %collective-permute-start = (bf16[2,256,128]{2,1,0:T(8,128)(2,1)S(1)}, bf16[2,256,128]{2,1,0:T(8,128)(2,1)S(1)}, u32[]{:S(2)}, u32[]{:S(2)}) collective-permute-start(bf16[2,256,128]{2,1,0:T(8,128)(2,1)S(1)} %get-tuple-element.232), channel_id=1, source_target_pairs={{0,1},{1,2},{2,3},{4,5},{5,6},{6,7},{8,9},{9,10},{10,11},{12,13},{... | collective-permute-start | bytes 393224 | tf_op jit(solution)/shard_map/while/body/eval_jaxpr/ppermute | solution.py:49
  342.4 1.9 collective-permute-done
  345.3 1.0 convolution_add_fusion.4
  (76 shorter events, 15.7 us)
Async XLA Ops:
  6.5 1.5 copy-start
  6.5 73.6 %all-gather.3.cloned.1.call-start = ((), (), s32[]{:S(2)}) async-start(), calls=%async_computation | async-start | bytes 2359296 | tf_op jit(solution)/shard_map/all_gather | solution.py:112
  7.3 302.1 %all-gather.5.cloned.1.call-start = ((), (), s32[]{:S(2)}) async-start(), calls=%async_computation.1 | async-start | bytes 18874368 | tf_op jit(solution)/shard_map/all_gather | solution.py:111
  8.0 13.0 %collective-permute-start.1 = (bf16[1024,128]{1,0:T(8,128)(2,1)S(1)}, bf16[1024,128]{1,0:T(8,128)(2,1)S(1)}, u32[]{:S(2)}, u32[]{:S(2)}) collective-permute-start(bf16[1024,128]{1,0:T(8,128)(2,1)S(1)} %copy-done), channel_id=1, source_target_pairs={{0,4},{4,8},{8,12},{12,16},{16,20},{20,24},{24,28},{28,0},{1,5},{5... | collective-permute-start | bytes 786440 | tf_op jit(solution)/shard_map/ppermute | solution.py:30
  10.1 26.9 %collective-permute-start.5 = (bf16[1024,128]{1,0:T(8,128)(2,1)S(1)}, bf16[1024,128]{1,0:T(8,128)(2,1)S(1)}, u32[]{:S(2)}, u32[]{:S(2)}) collective-permute-start(bf16[1024,128]{1,0:T(8,128)(2,1)S(1)} %copy-done), channel_id=1, source_target_pairs={{4,0},{8,4},{12,8},{16,12},{20,16},{24,20},{28,24},{0,28},{5,1},{9... | collective-permute-start | bytes 786440 | tf_op jit(solution)/shard_map/ppermute | solution.py:33
  13.3 39.6 %copy-start.2 = (bf16[8192]{0:T(1024)(128)(2,1)S(1)}, bf16[8192]{0:T(1024)(128)(2,1)}, u32[]{:S(2)}) copy-start(bf16[8192]{0:T(1024)(128)(2,1)} %param.11) | copy-start | bytes 49156
  13.3 39.6 %copy-start.3 = (bf16[1024]{0:T(1024)(128)(2,1)S(1)}, bf16[1024]{0:T(1024)(128)(2,1)}, u32[]{:S(2)}) copy-start(bf16[1024]{0:T(1024)(128)(2,1)} %param.15) | copy-start | bytes 6148
  13.3 39.6 %copy-start.4 = (bf16[128]{0:T(256)(128)(2,1)S(1)}, bf16[128]{0:T(256)(128)(2,1)}, u32[]{:S(2)}) copy-start(bf16[128]{0:T(256)(128)(2,1)} %param.16) | copy-start | bytes 772
  13.3 39.6 %copy-start.5 = (bf16[128]{0:T(256)(128)(2,1)S(1)}, bf16[128]{0:T(256)(128)(2,1)}, u32[]{:S(2)}) copy-start(bf16[128]{0:T(256)(128)(2,1)} %param.17) | copy-start | bytes 772
  21.0 16.1 %collective-permute-start.2 = (bf16[1024,128]{1,0:T(8,128)(2,1)S(1)}, bf16[1024,128]{1,0:T(8,128)(2,1)S(1)}, u32[]{:S(2)}, u32[]{:S(2)}) collective-permute-start(bf16[1024,128]{1,0:T(8,128)(2,1)S(1)} %collective-permute-done.1), channel_id=1, source_target_pairs={{0,4},{4,8},{8,12},{12,16},{16,20},{20,24},{24,28},{28,0},{1,5},{5... | collective-permute-start | bytes 786440 | tf_op jit(solution)/shard_map/ppermute | solution.py:30
  37.1 13.0 %collective-permute-start.3 = (bf16[1024,128]{1,0:T(8,128)(2,1)S(1)}, bf16[1024,128]{1,0:T(8,128)(2,1)S(1)}, u32[]{:S(2)}, u32[]{:S(2)}) collective-permute-start(bf16[1024,128]{1,0:T(8,128)(2,1)S(1)} %collective-permute-done.2), channel_id=1, source_target_pairs={{0,4},{4,8},{8,12},{12,16},{16,20},{20,24},{24,28},{28,0},{1,5},{5... | collective-permute-start | bytes 786440 | tf_op jit(solution)/shard_map/ppermute | solution.py:30
  37.1 16.5 %collective-permute-start.6 = (bf16[1024,128]{1,0:T(8,128)(2,1)S(1)}, bf16[1024,128]{1,0:T(8,128)(2,1)}, u32[]{:S(2)}, u32[]{:S(2)}) collective-permute-start(bf16[1024,128]{1,0:T(8,128)(2,1)S(1)} %collective-permute-done.5), channel_id=1, source_target_pairs={{4,0},{8,4},{12,8},{16,12},{20,16},{24,20},{28,24},{0,28},{5,1},{9... | collective-permute-start | bytes 786440 | tf_op jit(solution)/shard_map/ppermute | solution.py:33
  50.0 12.8 %copy-start.1 = (bf16[1024,128]{1,0:T(8,128)(2,1)}, bf16[1024,128]{1,0:T(8,128)(2,1)S(1)}, u32[]{:S(2)}) copy-start(bf16[1024,128]{1,0:T(8,128)(2,1)S(1)} %collective-permute-done.3) | copy-start | bytes 786436
  50.0 19.5 %collective-permute-start.4 = (bf16[1024,128]{1,0:T(8,128)(2,1)S(1)}, bf16[1024,128]{1,0:T(8,128)(2,1)}, u32[]{:S(2)}, u32[]{:S(2)}) collective-permute-start(bf16[1024,128]{1,0:T(8,128)(2,1)S(1)} %collective-permute-done.3), channel_id=1, source_target_pairs={{0,4},{4,8},{8,12},{12,16},{16,20},{20,24},{24,28},{28,0},{1,5},{5... | collective-permute-start | bytes 786440 | tf_op jit(solution)/shard_map/ppermute | solution.py:30
  53.6 19.5 %collective-permute-start.7 = (bf16[1024,128]{1,0:T(8,128)(2,1)}, bf16[1024,128]{1,0:T(8,128)(2,1)S(1)}, u32[]{:S(2)}, u32[]{:S(2)}) collective-permute-start(bf16[1024,128]{1,0:T(8,128)(2,1)} %collective-permute-done.6), channel_id=1, source_target_pairs={{4,0},{8,4},{12,8},{16,12},{20,16},{24,20},{28,24},{0,28},{5,1},{9... | collective-permute-start | bytes 786440 | tf_op jit(solution)/shard_map/ppermute | solution.py:33
  321.8 6.0 %collective-permute-start = (bf16[2,256,128]{2,1,0:T(8,128)(2,1)S(1)}, bf16[2,256,128]{2,1,0:T(8,128)(2,1)S(1)}, u32[]{:S(2)}, u32[]{:S(2)}) collective-permute-start(bf16[2,256,128]{2,1,0:T(8,128)(2,1)S(1)} %get-tuple-element.232), channel_id=1, source_target_pairs={{0,1},{1,2},{2,3},{4,5},{5,6},{6,7},{8,9},{9,10},{10,11},{12,13},{... | collective-permute-start | bytes 393224 | tf_op jit(solution)/shard_map/while/body/eval_jaxpr/ppermute | solution.py:49
  329.8 6.3 %collective-permute-start = (bf16[2,256,128]{2,1,0:T(8,128)(2,1)S(1)}, bf16[2,256,128]{2,1,0:T(8,128)(2,1)S(1)}, u32[]{:S(2)}, u32[]{:S(2)}) collective-permute-start(bf16[2,256,128]{2,1,0:T(8,128)(2,1)S(1)} %get-tuple-element.232), channel_id=1, source_target_pairs={{0,1},{1,2},{2,3},{4,5},{5,6},{6,7},{8,9},{9,10},{10,11},{12,13},{... | collective-permute-start | bytes 393224 | tf_op jit(solution)/shard_map/while/body/eval_jaxpr/ppermute | solution.py:49
  338.1 6.3 %collective-permute-start = (bf16[2,256,128]{2,1,0:T(8,128)(2,1)S(1)}, bf16[2,256,128]{2,1,0:T(8,128)(2,1)S(1)}, u32[]{:S(2)}, u32[]{:S(2)}) collective-permute-start(bf16[2,256,128]{2,1,0:T(8,128)(2,1)S(1)} %get-tuple-element.232), channel_id=1, source_target_pairs={{0,1},{1,2},{2,3},{4,5},{5,6},{6,7},{8,9},{9,10},{10,11},{12,13},{... | collective-permute-start | bytes 393224 | tf_op jit(solution)/shard_map/while/body/eval_jaxpr/ppermute | solution.py:49
Sparse Core Ops, SparseCore 0:
  9.5 70.6 all-gather.2
  82.3 226.9 all-gather.4
